TPU v7x, 256 devices: a whole 4x4x8 slice. The times are simulated.
256 devices in a mesh: seq: 32 (over z_hi, x, core), uly: 8 (over y, z_lo).
Axes of the slice: x: 4, y: 4, z: 8 (z_hi: 4, z_lo: 2; z = z_hi * 2 + z_lo), core: 2. Of those that a mesh axis runs over, the one named last changes fastest.
Arguments:
- normed: bfloat16 [32768, 5376], P('seq', 'uly'), may hold values from -6 to 6
- q_raw: bfloat16 [32768, 2048], P('seq', 'uly'), may hold values from -6 to 6
- key_weight: bfloat16 [5376, 1024], P('uly', 'seq'), may hold values from -0.078125 to 0.078125
- value_weight: bfloat16 [5376, 1024], P('uly', 'seq'), may hold values from -0.078125 to 0.078125
- q_gain: float32 [128], replicated, may hold values from 0.1 to 1.9
- k_gain: float32 [128], replicated, may hold values from 0.1 to 1.9
- segment_ids: int32 [32768], replicated, may hold values from 0 to 1, as said below
- grad_out: bfloat16 [32768, 2048], P('seq', 'uly'), may hold values from -6 to 6
Outputs:
- attention: bfloat16 [32768, 2048], P('seq', 'uly')
- grad_normed: bfloat16 [32768, 5376], P('seq', 'uly')
- grad_q: bfloat16 [32768, 2048], P('seq', 'uly')
- grad_key_weight: float32 [5376, 1024], P('uly', 'seq')
- grad_value_weight: float32 [5376, 1024], P('uly', 'seq')
Inputs may be any that keep to these rules, and one draw needn't show every extreme that they name: `segment_ids`: 0 up to one position and 1 from it on; that position lies between 8192 and 24576.
All inputs are finite; a program needn't handle non-finite values.
Results may differ from a plain program's by a relative error of at most 0.025.
Values may be sent and summed in bfloat16 or wider, within the bound.
A program may use at most 128 MiB of HBM per device.

v0:
```python
import jax
import jax.numpy as jnp
from jax import lax
from jax.sharding import PartitionSpec as P

HD = 128
WINDOW = 1024
epsilon = 1e-06
query_scale = 168.0 ** (-0.5)


def from_behind(array, axis, by):
    devices = lax.axis_size(axis)
    pairs = [(i, i + by) for i in range(devices) if 0 <= i + by < devices]
    return lax.ppermute(array, axis, pairs)


def normalize(raw_vals, gain, factor):
    mean_sq = jnp.mean(raw_vals * raw_vals, axis=-1, keepdims=True)
    return raw_vals * lax.rsqrt(mean_sq + epsilon) * gain * factor


def attend_block(
    queries, key_block, value_block, grad_block, query_pos, key_pos, query_seg, key_seg
):
    scores = jnp.einsum("bhge,lhe->hgbl", queries, key_block, preferred_element_type=jnp.float32)
    allowed = (
        (key_pos[None, :] <= query_pos[:, None])
        & (key_pos[None, :] > query_pos[:, None] - WINDOW)
        & (key_seg[None, :] == query_seg[:, None])
    )
    exp_scores = jnp.where(allowed[None, None], jnp.exp(scores), 0.0)
    probs = exp_scores / jnp.sum(exp_scores, axis=-1, keepdims=True)
    weights = probs.astype(jnp.bfloat16)
    attended = jnp.einsum(
        "hgbl,lhe->bhge", weights, value_block, preferred_element_type=jnp.float32
    ).astype(jnp.bfloat16)
    dprob = jnp.einsum(
        "bhge,lhe->hgbl", grad_block, value_block, preferred_element_type=jnp.float32
    )
    delta_row = jnp.sum(probs * dprob, axis=-1, keepdims=True)
    dscore = (probs * (dprob - delta_row)).astype(jnp.bfloat16)
    dquery = jnp.einsum("hgbl,lhe->bhge", dscore, key_block, preferred_element_type=jnp.float32)
    dkey = jnp.einsum("hgbl,bhge->lhe", dscore, queries, preferred_element_type=jnp.float32)
    dvalue = jnp.einsum("hgbl,bhge->lhe", weights, grad_block, preferred_element_type=jnp.float32)
    return (attended, dquery, dkey, dvalue)


def body(normed, q_raw, key_weight, value_weight, q_gain, k_gain, segment_ids, grad_out):
    rows_here = normed.shape[0]
    heads_here = q_raw.shape[1] // (2 * HD)
    seq_index = lax.axis_index("seq")
    base_row = seq_index * rows_here
    weight_pair = (
        lax.all_gather(key_weight, "seq", axis=1, tiled=True),
        lax.all_gather(value_weight, "seq", axis=1, tiled=True),
    )
    key_term = jnp.dot(normed, weight_pair[0], preferred_element_type=jnp.float32)
    value_term = jnp.dot(normed, weight_pair[1], preferred_element_type=jnp.float32)
    key_raw, value_raw = (
        lax.psum_scatter(
            key_term.astype(jnp.bfloat16), "uly", scatter_dimension=1, tiled=True
        ).astype(jnp.float32),
        lax.psum_scatter(
            value_term.astype(jnp.bfloat16), "uly", scatter_dimension=1, tiled=True
        ).astype(jnp.float32),
    )
    key_in = key_raw.reshape(rows_here, heads_here, HD)
    keys_bf = normalize(key_in, k_gain, 1.0).astype(jnp.bfloat16)
    values_bf = value_raw.reshape(rows_here, heads_here, HD).astype(jnp.bfloat16)
    query_in = q_raw.astype(jnp.float32).reshape(rows_here, heads_here, 2, HD)
    queries = normalize(query_in, q_gain, query_scale).astype(jnp.bfloat16)
    grad_heads = grad_out.reshape(rows_here, heads_here, 2, HD)
    stacked = jnp.stack([keys_bf, values_bf])
    pieces = []
    distance = 1
    pieces.append(from_behind(stacked, "seq", distance))
    pieces.append(stacked)
    extended = jnp.concatenate(pieces, axis=1)
    block_rows = min(512, rows_here)
    span_rows = block_rows + WINDOW
    count_blocks = rows_here // block_rows
    seg_pad = jnp.concatenate([jnp.full((WINDOW,), -1, jnp.int32), segment_ids])
    query_seg_all = lax.dynamic_slice_in_dim(segment_ids, base_row, rows_here, 0)
    key_seg_all = lax.dynamic_slice_in_dim(seg_pad, base_row, WINDOW + rows_here, 0)

    def step(grad_acc, block_index):
        begin_row = block_index * block_rows
        query_pos = base_row + begin_row + jnp.arange(block_rows, dtype=jnp.int32)
        key_pos = base_row + begin_row - WINDOW + jnp.arange(span_rows, dtype=jnp.int32)
        key_block = lax.dynamic_slice_in_dim(extended, begin_row, span_rows, 1)
        attended, dquery, dkey, dvalue = attend_block(
            lax.dynamic_slice_in_dim(queries, begin_row, block_rows, 0),
            key_block[0],
            key_block[1],
            lax.dynamic_slice_in_dim(grad_heads, begin_row, block_rows, 0),
            query_pos,
            key_pos,
            lax.dynamic_slice_in_dim(query_seg_all, begin_row, block_rows, 0),
            lax.dynamic_slice_in_dim(key_seg_all, begin_row, span_rows, 0),
        )
        update = jnp.stack([dkey, dvalue])
        grad_acc = lax.dynamic_update_slice_in_dim(
            grad_acc,
            lax.dynamic_slice_in_dim(grad_acc, begin_row, span_rows, 1) + update,
            begin_row,
            1,
        )
        return (grad_acc, (attended, dquery))

    zero_acc = jnp.zeros((2, WINDOW + rows_here, heads_here, HD), jnp.float32)
    grad_acc, (attended, dquery) = lax.scan(
        step, zero_acc, jnp.arange(count_blocks, dtype=jnp.int32)
    )
    attention = attended.reshape(rows_here, 2 * heads_here * HD)
    dquery = dquery.reshape(rows_here, heads_here, 2, HD)
    own_grads = grad_acc[:, WINDOW:]
    offset_row = 0
    distance = 1
    first_row = max(0, distance * rows_here - WINDOW)
    piece_rows = rows_here - first_row
    outgoing = grad_acc[:, offset_row : offset_row + piece_rows]
    returned = from_behind(outgoing.astype(jnp.bfloat16), "seq", -distance).astype(outgoing.dtype)
    own_grads = own_grads.at[:, first_row:].add(returned)
    _, pull_query = jax.vjp(lambda raw_vals: normalize(raw_vals, q_gain, query_scale), query_in)
    grad_q = pull_query(dquery)[0].astype(jnp.bfloat16).reshape(rows_here, 2 * heads_here * HD)
    _, pull_key = jax.vjp(lambda raw_vals: normalize(raw_vals, k_gain, 1.0), key_in)
    key_grad = pull_key(own_grads[0])[0].astype(jnp.bfloat16).reshape(rows_here, heads_here * HD)
    value_grad = own_grads[1].astype(jnp.bfloat16).reshape(rows_here, heads_here * HD)
    key_all, value_all = (
        lax.all_gather(key_grad, "uly", axis=1, tiled=True),
        lax.all_gather(value_grad, "uly", axis=1, tiled=True),
    )
    dims_last = (((1,), (1,)), ((), ()))
    total = lax.dot_general(key_all, weight_pair[0], dims_last, preferred_element_type=jnp.float32)
    total = total + lax.dot_general(
        value_all, weight_pair[1], dims_last, preferred_element_type=jnp.float32
    )
    grad_normed = total.astype(jnp.bfloat16)
    dims_first = (((0,), (0,)), ((), ()))
    key_part = lax.dot_general(normed, key_all, dims_first, preferred_element_type=jnp.float32)
    value_part = lax.dot_general(normed, value_all, dims_first, preferred_element_type=jnp.float32)
    grad_key_weight = lax.psum_scatter(
        key_part.astype(jnp.bfloat16), "seq", scatter_dimension=1, tiled=True
    ).astype(jnp.float32)
    grad_value_weight = lax.psum_scatter(
        value_part.astype(jnp.bfloat16), "seq", scatter_dimension=1, tiled=True
    ).astype(jnp.float32)
    return (attention, grad_normed, grad_q, grad_key_weight, grad_value_weight)


def solution(mesh):
    return jax.shard_map(
        body,
        mesh=mesh,
        in_specs=(
            P("seq", "uly"),
            P("seq", "uly"),
            P("uly", "seq"),
            P("uly", "seq"),
            P(),
            P(),
            P(),
            P("seq", "uly"),
        ),
        out_specs=(
            P("seq", "uly"),
            P("seq", "uly"),
            P("seq", "uly"),
            P("uly", "seq"),
            P("uly", "seq"),
        ),
        check_vma=False,
    )
```

profile of v0, /device:TPU:8, one launch (start us, length us, event | category | flops | bytes accessed | tf_op | source)
XLA Modules:
  0.0 660.0 jit_solution(17294904801628966147)
XLA Ops:
  8.7 57.9 %all-gather.6.cloned.1.call-done = bf16[672,1024]{0,1:T(8,128)(2,1)} async-done(((bf16[672,32]{0,1:T(8,128)(2,1)}), bf16[672,1024]{0,1:T(8,128)(2,1)}) %all-gather.6.cloned.1.call-update) | async-done | bytes 1376272 | tf_op jit(solution)/shard_map/all_gather | solution.py:55
  66.6 3.3 convolution_convert_fusion.1
  72.5 46.9 %all-gather.8.cloned.1.call-done = bf16[672,1024]{0,1:T(8,128)(2,1)} async-done(((bf16[672,32]{0,1:T(8,128)(2,1)}), bf16[672,1024]{0,1:T(8,128)(2,1)}) %all-gather.8.cloned.1.call-update) | async-done | bytes 1376272 | tf_op jit(solution)/shard_map/all_gather | solution.py:56
  119.5 3.3 convolution_convert_fusion
  126.8 45.8 %reduce-scatter.13.cloned.1.call-done = bf16[128,1024]{1,0:T(8,128)(2,1)} async-done(((bf16[1024,1024]{1,0:T(8,128)(2,1)}), bf16[128,1024]{1,0:T(8,128)(2,1)}) %reduce-scatter.13.cloned.1.call-update) | async-done | bytes 262160
  174.0 55.4 %reduce-scatter.15.cloned.1.call-done = bf16[128,1024]{1,0:T(8,128)(2,1)} async-done(((bf16[1024,1024]{1,0:T(8,128)(2,1)}), bf16[128,1024]{1,0:T(8,128)(2,1)}) %reduce-scatter.15.cloned.1.call-update) | async-done | bytes 262160
  243.2 79.3 %while.19 = (s32[]{:T(128)}, f32[2,2048,1,128]{3,1,2,0:T(8,128)}, bf16[2,512,1,2,128]{4,3,1,0,2:T(2,128)(2,1)}, f32[2,512,1,2,128]{1,4,3,2,0:T(8,128)}, s32[2]{0...) while((s32[]{:T(128)}, f32[2,2048,1,128]{3,1,2,0:T(8,128)}, ...), condition=%wide.region_7.8_spmd, body=%wide.region_4.7_spmd.sunk | while | flops 2447507968 | bytes 149759104 | solution.py:112
  245.5 5.4 fusion.90
  251.0 5.3 fusion.92
  258.3 3.2 convolution_bitcast_fusion.3
  276.9 4.7 fusion.94
  285.2 5.4 fusion.90
  290.7 5.3 fusion.92
  298.0 3.2 convolution_bitcast_fusion.3
  316.6 4.7 fusion.94
  325.4 5.3 collective-permute-done.1
  334.2 74.7 %all-gather.10.cloned.1.call-done = bf16[1024,1024]{1,0:T(8,128)(2,1)} async-done(((bf16[1024,128]{1,0:T(8,128)(2,1)}), bf16[1024,1024]{1,0:T(8,128)(2,1)}) %all-gather.10.cloned.1.call-update) | async-done | bytes 2097168 | tf_op jit(solution)/shard_map/all_gather | solution.py:131
  408.9 3.2 fusion.46
  413.7 51.5 %all-gather.12.cloned.1.call-done = bf16[1,1024,1,1024]{3,1,2,0:T(8,128)(2,1)} async-done(((bf16[1,1024,1,128]{3,1,2,0:T(8,128)(2,1)}), bf16[1,1024,1,1024]{3,1,2,0:T(8,128)(2,1)}) %all-gather.12.cloned.1.call-update) | async-done | bytes 2097168 | tf_op jit(solution)/shard_map/all_gather | solution.py:132
  465.2 4.3 fusion.47
  480.8 3.9 fusion.41
  484.7 2.7 add_convert_fusion
  487.5 72.3 %reduce-scatter.17.cloned.1.call-done = bf16[32,672]{1,0:T(8,128)(2,1)} async-done(((bf16[1024,672]{1,0:T(8,128)(2,1)}), bf16[32,672]{1,0:T(8,128)(2,1)}) %reduce-scatter.17.cloned.1.call-update) | async-done | bytes 43024
  561.5 89.9 %reduce-scatter.19.cloned.1.call-done = bf16[32,672]{1,0:T(8,128)(2,1)} async-done(((bf16[1024,672]{1,0:T(8,128)(2,1)}), bf16[32,672]{1,0:T(8,128)(2,1)}) %reduce-scatter.19.cloned.1.call-update) | async-done | bytes 43024
  (190 shorter events, 86.4 us)
Async XLA Ops:
  7.2 59.4 %copy-start = (bf16[1024,672]{0,1:T(8,128)(2,1)S(1)}, bf16[1024,672]{0,1:T(8,128)(2,1)}, u32[]{:S(2)}) copy-start(bf16[1024,672]{0,1:T(8,128)(2,1)} %param.14) | copy-start | bytes 4128772
  7.2 59.4 %all-gather.6.cloned.1.call-start = ((), (), s32[]{:S(2)}) async-start(), calls=%async_computation.4 | async-start | bytes 1622016 | tf_op jit(solution)/shard_map/all_gather | solution.py:55
  7.9 111.6 %all-gather.8.cloned.1.call-start = ((), (), s32[]{:S(2)}) async-start(), calls=%async_computation.5 | async-start | bytes 1622016 | tf_op jit(solution)/shard_map/all_gather | solution.py:56
  8.7 163.9 %reduce-scatter.13.cloned.1.call-start = ((), (), s32[]{:S(2)}) async-start(), calls=%async_computation.8 | async-start | bytes 2359296
  72.5 156.9 %reduce-scatter.15.cloned.1.call-start = ((), (), s32[]{:S(2)}) async-start(), calls=%async_computation.9 | async-start | bytes 2359296
  125.3 283.5 %all-gather.10.cloned.1.call-start = ((), (), s32[]{:S(2)}) async-start(), calls=%async_computation.6 | async-start | bytes 2359296 | tf_op jit(solution)/shard_map/all_gather | solution.py:131
  126.6 112.0 %copy-start.9 = (bf16[1024,256]{0,1:T(8,128)(2,1)}, bf16[1024,256]{0,1:T(8,128)(2,1)S(1)}, u32[]{:S(2)}) copy-start(bf16[1024,256]{0,1:T(8,128)(2,1)S(1)} %copy.78) | copy-start | bytes 1572868
  126.6 104.6 %copy-start.27 = (f32[128]{0:T(128)S(1)}, f32[128]{0:T(128)}, u32[]{:S(2)}) copy-start(f32[128]{0:T(128)} %param.19) | copy-start | bytes 1540
  126.7 111.8 %copy-start.7 = (f32[1024,256]{0,1:T(8,128)}, f32[1024,256]{0,1:T(8,128)S(1)}, u32[]{:S(2)}) copy-start(f32[1024,256]{0,1:T(8,128)S(1)} %convert_element_type.99) | copy-start | bytes 3145732
  126.8 111.7 %copy-start.21 = (f32[1024,2]{0,1:T(2,128)}, f32[1024,2]{0,1:T(2,128)S(1)}, u32[]{:S(2)}) copy-start(f32[1024,2]{0,1:T(2,128)S(1)} %multiply_reduce_fusion.1) | copy-start | bytes 24580
  126.8 111.7 %copy-start.29 = (f32[128]{0:T(128)S(1)}, f32[128]{0:T(128)}, u32[]{:S(2)}) copy-start(f32[128]{0:T(128)} %param.18) | copy-start | bytes 1540
  173.7 65.8 %copy-start.11 = (bf16[1024,128]{1,0:T(8,128)(2,1)}, bf16[1024,128]{1,0:T(8,128)(2,1)S(1)}, u32[]{:S(2)}) copy-start(bf16[1024,128]{1,0:T(8,128)(2,1)S(1)} %copy.102) | copy-start | bytes 786436
  174.0 59.2 %copy-start.25 = (f32[1024]{0:T(1024)}, f32[1024]{0:T(1024)S(1)}, u32[]{:S(2)}) copy-start(f32[1024]{0:T(1024)S(1)} %fusion.52) | copy-start | bytes 12292
  174.0 59.2 %copy-start.23 = (f32[1024]{0:T(1024)}, f32[1024]{0:T(1024)S(1)}, u32[]{:S(2)}) copy-start(f32[1024]{0:T(1024)S(1)} %fusion.59) | copy-start | bytes 12292
  233.2 6.4 collective-permute-start
  245.5 5.4 copy-start.3
  322.5 9.5 %copy-start.12 = (bf16[1024,128]{1,0:T(8,128)(2,1)S(1)}, bf16[1024,128]{1,0:T(8,128)(2,1)}, u32[]{:S(2)}) copy-start(bf16[1024,128]{1,0:T(8,128)(2,1)} %copy-done.11) | copy-start | bytes 786436
  322.5 9.5 %copy-start.28 = (f32[128]{0:T(128)S(1)}, f32[128]{0:T(128)}, u32[]{:S(2)}) copy-start(f32[128]{0:T(128)} %param.19) | copy-start | bytes 1540
  322.5 9.7 %copy-start.26 = (f32[1024]{0:T(1024)S(1)}, f32[1024]{0:T(1024)}, u32[]{:S(2)}) copy-start(f32[1024]{0:T(1024)} %copy-done.25) | copy-start | bytes 12292
  322.5 9.8 %copy-start.24 = (f32[1024]{0:T(1024)S(1)}, f32[1024]{0:T(1024)}, u32[]{:S(2)}) copy-start(f32[1024]{0:T(1024)} %copy-done.23) | copy-start | bytes 12292
  323.9 6.8 %collective-permute-start.1 = (bf16[2,1024,1,128]{3,1,2,0:T(8,128)(2,1)S(1)}, bf16[2,1024,1,128]{3,1,2,0:T(8,128)(2,1)S(1)}, u32[]{:S(2)}, u32[]{:S(2)}) collective-permute-start(bf16[2,1024,1,128]{3,1,2,0:T(8,128)(2,1)S(1)} %slice.69), channel_id=1, source_target_pairs={{8,0},{16,8},{24,16},{32,24},{40,32},{48,40},{56,48},{64,56},{72,6... | collective-permute-start | bytes 1572872 | tf_op jit(solution)/shard_map/ppermute | solution.py:15
  333.4 131.8 %all-gather.12.cloned.1.call-start = ((), (), s32[]{:S(2)}) async-start(), calls=%async_computation.7 | async-start | bytes 2359296 | tf_op jit(solution)/shard_map/all_gather | solution.py:132
  334.2 225.7 %reduce-scatter.17.cloned.1.call-start = ((), (), s32[]{:S(2)}) async-start(), calls=%async_computation.10 | async-start | bytes 1622016
  413.7 237.8 %reduce-scatter.19.cloned.1.call-start = ((), (), s32[]{:S(2)}) async-start(), calls=%async_computation.11 | async-start | bytes 1622016
  (33 other events, 105.4 us)
Sparse Core Ops, SparseCore 0:
  10.6 55.9 all-gather.5
  69.1 50.2 all-gather.7
  122.0 50.5 reduce-scatter.12
  175.0 54.3 reduce-scatter.14
  333.5 75.3 all-gather.9
  411.0 54.1 all-gather.11
  469.0 90.7 reduce-scatter.16
  563.6 87.7 reduce-scatter.18
where the time goes:
time: 661 us; the launch traced here: 660 us
  waiting for transfers between devices  501 us (76%)
  matrix products  68.2 us (10%)
  local copies, waits for them, and re-layouts  50 us (8%)
  other arithmetic  20.2 us (3%)
  between operations  14.5 us (2%)
    unnamed x12, waiting for transfers between devices  265 us
    all_gather x1, waiting for transfers between devices, body(): lax.all_gather(key_grad, 'uly', axis=1, tiled=True)  74.7 us
    all_gather x1, waiting for transfers between devices, body(): lax.all_gather(key_weight, 'seq', axis=1, tiled=True)  57.9 us
    all_gather x1, waiting for transfers between devices, body(): lax.all_gather(value_grad, 'uly', axis=1, tiled=True)  51.5 us
    all_gather x1, waiting for transfers between devices, body(): lax.all_gather(value_weight, 'seq', axis=1, tiled=True)  46.9 us
    unnamed x63, local copies, waits for them, and re-layouts  22.4 us
  transfers between devices with their start and end apart: 10, of which 9 were waited for; matrix products, arithmetic and copies ran while one was open for 7% of the time, Pallas kernels for 0%

commit v1 on v0

--- a/solution.py
+++ b/solution.py
@@ -127,8 +127,17 @@
     _, pull_key = jax.vjp(lambda raw_vals: normalize(raw_vals, k_gain, 1.0), key_in)
     key_grad = pull_key(own_grads[0])[0].astype(jnp.bfloat16).reshape(rows_here, heads_here * HD)
     value_grad = own_grads[1].astype(jnp.bfloat16).reshape(rows_here, heads_here * HD)
+    change_stocks_by_axis = lambda view: jnp.concatenate(
+        lax.all_to_all(
+            jnp.stack([view for _ in range(lax.axis_size("uly"))]),
+            axis_name="uly",
+            split_axis=0,
+            concat_axis=0,
+        ),
+        axis=1,
+    )
     key_all, value_all = (
-        lax.all_gather(key_grad, "uly", axis=1, tiled=True),
+        change_stocks_by_axis(key_grad),
         lax.all_gather(value_grad, "uly", axis=1, tiled=True),
     )
     dims_last = (((1,), (1,)), ((), ()))

time: 661 us -> 614 us (0.929)
  waiting for transfers between devices: 501 us -> 445 us
    all_gather x1 -> x0, waiting for transfers between devices: 74.7 us -> none  [body(): lax.all_gather(key_grad, 'uly', axis=1, tiled=True)]
    all_to_all x0 -> x1, waiting for transfers between devices: none -> 19.7 us  [body(): lax.all_to_all(jnp.stack([view for _ in range(lax.axis_size('uly'))]), ax...]
    unnamed x12 -> x11, waiting for transfers between devices: 265 us -> 263 us
    unnamed x63 -> x61, local copies, waits for them, and re-layouts: 22.4 us -> 22.4 us
  transfers between devices with their start and end apart: 10 -> 10, of which waited for: 9 -> 9; matrix products, arithmetic and copies ran while one was open for 7% -> 8% of each run, Pallas kernels for 0% -> 0%
where the time goes in v1:
time: 614 us; the launch traced here: 613 us
  waiting for transfers between devices  445 us (72%)
  matrix products  69.8 us (11%)
  local copies, waits for them, and re-layouts  51.9 us (8%)
  other arithmetic  19.5 us (3%)
  between operations  14.5 us (2%)
  starting transfers between devices  10.8 us (2%)
    unnamed x11, waiting for transfers between devices  263 us
    all_gather x1, waiting for transfers between devices, body(): lax.all_gather(key_weight, 'seq', axis=1, tiled=True)  57.9 us
    all_gather x1, waiting for transfers between devices, body(): lax.all_gather(value_grad, 'uly', axis=1, tiled=True)  52.2 us
    all_gather x1, waiting for transfers between devices, body(): lax.all_gather(value_weight, 'seq', axis=1, tiled=True)  46.9 us
    unnamed x61, local copies, waits for them, and re-layouts  22.4 us
    all_to_all x1, waiting for transfers between devices, body(): lax.all_to_all(jnp.stack([view for _ in range(lax.axis_size('uly'))]), ax...  19.7 us
  transfers between devices with their start and end apart: 10, of which 9 were waited for; matrix products, arithmetic and copies ran while one was open for 8% of the time, Pallas kernels for 0%

profile of v1, /device:TPU:8, one launch (start us, length us, event | category | flops | bytes accessed | tf_op | source)
XLA Modules:
  0.0 613.2 jit_solution(3578456708252960661)
XLA Ops:
  8.7 57.9 %all-gather.5.cloned.1.call-done = bf16[672,1024]{0,1:T(8,128)(2,1)} async-done(((bf16[672,32]{0,1:T(8,128)(2,1)}), bf16[672,1024]{0,1:T(8,128)(2,1)}) %all-gather.5.cloned.1.call-update) | async-done | bytes 1376272 | tf_op jit(solution)/shard_map/all_gather | solution.py:55
  66.6 3.3 convolution_convert_fusion.1
  72.5 46.9 %all-gather.7.cloned.1.call-done = bf16[672,1024]{0,1:T(8,128)(2,1)} async-done(((bf16[672,32]{0,1:T(8,128)(2,1)}), bf16[672,1024]{0,1:T(8,128)(2,1)}) %all-gather.7.cloned.1.call-update) | async-done | bytes 1376272 | tf_op jit(solution)/shard_map/all_gather | solution.py:56
  119.5 3.3 convolution_convert_fusion
  126.8 45.8 %reduce-scatter.13.cloned.1.call-done = bf16[128,1024]{1,0:T(8,128)(2,1)} async-done(((bf16[1024,1024]{1,0:T(8,128)(2,1)}), bf16[128,1024]{1,0:T(8,128)(2,1)}) %reduce-scatter.13.cloned.1.call-update) | async-done | bytes 262160
  174.0 55.4 %reduce-scatter.15.cloned.1.call-done = bf16[128,1024]{1,0:T(8,128)(2,1)} async-done(((bf16[1024,1024]{1,0:T(8,128)(2,1)}), bf16[128,1024]{1,0:T(8,128)(2,1)}) %reduce-scatter.15.cloned.1.call-update) | async-done | bytes 262160
  243.2 79.5 %while.19 = (s32[]{:T(128)}, f32[2,2048,1,128]{3,1,2,0:T(8,128)}, bf16[2,512,1,2,128]{4,3,1,0,2:T(2,128)(2,1)}, f32[2,512,1,2,128]{1,4,3,2,0:T(8,128)}, s32[2]{0...) while((s32[]{:T(128)}, f32[2,2048,1,128]{3,1,2,0:T(8,128)}, ...), condition=%wide.region_7.8_spmd, body=%wide.region_4.7_spmd.sunk | while | flops 2447507968 | bytes 149759104 | solution.py:112
  245.6 5.4 fusion.90
  251.1 5.2 fusion.92
  258.4 3.2 convolution_bitcast_fusion.3
  277.0 4.7 fusion.94
  285.4 5.4 fusion.90
  290.8 5.3 fusion.92
  298.1 3.2 convolution_bitcast_fusion.3
  316.7 4.7 fusion.94
  325.5 5.3 collective-permute-done.1
  334.6 6.5 %all-to-all-start = ((bf16[8,1024,128]{1,2,0:T(8,128)(2,1)}), bf16[8,1024,128]{1,2,0:T(8,128)(2,1)}, u32[]{:S(2)}, u32[]{:S(2)}) async-start(bf16[8,1024,128]{1,2,0:T(8,128)(2,1)} %stack.36), calls=%async_computation | async-start | bytes 4194304 | tf_op jit(solution)/shard_map/all_to_all | solution.py:131
  341.8 19.7 %all-to-all-done = bf16[8,1024,128]{1,2,0:T(8,128)(2,1)} async-done(((bf16[8,1024,128]{1,2,0:T(8,128)(2,1)}), bf16[8,1024,128]{1,2,0:T(8,128)(2,1)}, u32[]{:S(2)}, u32[]{:S(2)}) %all-to-all-start) | async-done | bytes 2097184 | tf_op jit(solution)/shard_map/all_to_all | solution.py:131
  366.3 52.2 %all-gather.9.cloned.1.call-done = bf16[1,1024,1,1024]{3,1,2,0:T(8,128)(2,1)} async-done(((bf16[1,1024,1,128]{3,1,2,0:T(8,128)(2,1)}), bf16[1,1024,1,1024]{3,1,2,0:T(8,128)(2,1)}) %all-gather.9.cloned.1.call-update) | async-done | bytes 2097168 | tf_op jit(solution)/shard_map/all_gather | solution.py:141
  418.6 4.3 fusion.47
  434.2 3.9 fusion.41
  438.1 4.4 add_convert_fusion
  442.5 70.5 %reduce-scatter.17.cloned.1.call-done = bf16[32,672]{1,0:T(8,128)(2,1)} async-done(((bf16[1024,672]{1,0:T(8,128)(2,1)}), bf16[32,672]{1,0:T(8,128)(2,1)}) %reduce-scatter.17.cloned.1.call-update) | async-done | bytes 43024
  514.8 89.8 %reduce-scatter.19.cloned.1.call-done = bf16[32,672]{1,0:T(8,128)(2,1)} async-done(((bf16[1024,672]{1,0:T(8,128)(2,1)}), bf16[32,672]{1,0:T(8,128)(2,1)}) %reduce-scatter.19.cloned.1.call-update) | async-done | bytes 43024
  (189 shorter events, 90.7 us)
Async XLA Ops:
  7.2 59.4 %copy-start = (bf16[1024,672]{0,1:T(8,128)(2,1)S(1)}, bf16[1024,672]{0,1:T(8,128)(2,1)}, u32[]{:S(2)}) copy-start(bf16[1024,672]{0,1:T(8,128)(2,1)} %param.14) | copy-start | bytes 4128772
  7.2 59.4 %all-gather.5.cloned.1.call-start = ((), (), s32[]{:S(2)}) async-start(), calls=%async_computation.5 | async-start | bytes 1622016 | tf_op jit(solution)/shard_map/all_gather | solution.py:55
  7.9 111.6 %all-gather.7.cloned.1.call-start = ((), (), s32[]{:S(2)}) async-start(), calls=%async_computation.6 | async-start | bytes 1622016 | tf_op jit(solution)/shard_map/all_gather | solution.py:56
  8.7 163.9 %reduce-scatter.13.cloned.1.call-start = ((), (), s32[]{:S(2)}) async-start(), calls=%async_computation.8 | async-start | bytes 2359296
  72.5 156.9 %reduce-scatter.15.cloned.1.call-start = ((), (), s32[]{:S(2)}) async-start(), calls=%async_computation.9 | async-start | bytes 2359296
  126.6 112.0 %copy-start.9 = (bf16[1024,256]{0,1:T(8,128)(2,1)}, bf16[1024,256]{0,1:T(8,128)(2,1)S(1)}, u32[]{:S(2)}) copy-start(bf16[1024,256]{0,1:T(8,128)(2,1)S(1)} %copy.80) | copy-start | bytes 1572868
  126.6 104.6 %copy-start.27 = (f32[128]{0:T(128)S(1)}, f32[128]{0:T(128)}, u32[]{:S(2)}) copy-start(f32[128]{0:T(128)} %param.19) | copy-start | bytes 1540
  126.7 111.8 %copy-start.7 = (f32[1024,256]{0,1:T(8,128)}, f32[1024,256]{0,1:T(8,128)S(1)}, u32[]{:S(2)}) copy-start(f32[1024,256]{0,1:T(8,128)S(1)} %convert_element_type.99) | copy-start | bytes 3145732
  126.8 111.7 %copy-start.21 = (f32[1024,2]{0,1:T(2,128)}, f32[1024,2]{0,1:T(2,128)S(1)}, u32[]{:S(2)}) copy-start(f32[1024,2]{0,1:T(2,128)S(1)} %multiply_reduce_fusion.1) | copy-start | bytes 24580
  126.8 111.7 %copy-start.29 = (f32[128]{0:T(128)S(1)}, f32[128]{0:T(128)}, u32[]{:S(2)}) copy-start(f32[128]{0:T(128)} %param.18) | copy-start | bytes 1540
  173.7 65.8 %copy-start.11 = (bf16[1024,128]{1,0:T(8,128)(2,1)}, bf16[1024,128]{1,0:T(8,128)(2,1)S(1)}, u32[]{:S(2)}) copy-start(bf16[1024,128]{1,0:T(8,128)(2,1)S(1)} %copy.105) | copy-start | bytes 786436
  174.0 59.2 %copy-start.25 = (f32[1024]{0:T(1024)}, f32[1024]{0:T(1024)S(1)}, u32[]{:S(2)}) copy-start(f32[1024]{0:T(1024)S(1)} %fusion.52) | copy-start | bytes 12292
  174.0 59.2 %copy-start.23 = (f32[1024]{0:T(1024)}, f32[1024]{0:T(1024)S(1)}, u32[]{:S(2)}) copy-start(f32[1024]{0:T(1024)S(1)} %fusion.59) | copy-start | bytes 12292
  233.2 6.4 %collective-permute-start = (bf16[2,1024,1,128]{3,1,2,0:T(8,128)(2,1)}, bf16[2,1024,1,128]{3,1,2,0:T(8,128)(2,1)}, u32[]{:S(2)}, u32[]{:S(2)}) collective-permute-start(bf16[2,1024,1,128]{3,1,2,0:T(8,128)(2,1)} %pad_maximum_fusion), channel_id=1, source_target_pairs={{0,8},{8,16},{16,24},{24,32},{32,40},{40,48},{48,56},{56,64},{64,7... | collective-permute-start | bytes 1572872 | tf_op jit(solution)/shard_map/ppermute | solution.py:15
  285.4 5.4 copy-start.3
  322.6 9.5 %copy-start.12 = (bf16[1024,128]{1,0:T(8,128)(2,1)S(1)}, bf16[1024,128]{1,0:T(8,128)(2,1)}, u32[]{:S(2)}) copy-start(bf16[1024,128]{1,0:T(8,128)(2,1)} %copy-done.11) | copy-start | bytes 786436
  322.6 9.5 %copy-start.28 = (f32[128]{0:T(128)S(1)}, f32[128]{0:T(128)}, u32[]{:S(2)}) copy-start(f32[128]{0:T(128)} %param.19) | copy-start | bytes 1540
  322.6 9.7 %copy-start.26 = (f32[1024]{0:T(1024)S(1)}, f32[1024]{0:T(1024)}, u32[]{:S(2)}) copy-start(f32[1024]{0:T(1024)} %copy-done.25) | copy-start | bytes 12292
  322.7 9.8 %copy-start.24 = (f32[1024]{0:T(1024)S(1)}, f32[1024]{0:T(1024)}, u32[]{:S(2)}) copy-start(f32[1024]{0:T(1024)} %copy-done.23) | copy-start | bytes 12292
  324.0 6.8 %collective-permute-start.1 = (bf16[2,1024,1,128]{3,1,2,0:T(8,128)(2,1)S(1)}, bf16[2,1024,1,128]{3,1,2,0:T(8,128)(2,1)S(1)}, u32[]{:S(2)}, u32[]{:S(2)}) collective-permute-start(bf16[2,1024,1,128]{3,1,2,0:T(8,128)(2,1)S(1)} %slice.69), channel_id=1, source_target_pairs={{8,0},{16,8},{24,16},{32,24},{40,32},{48,40},{56,48},{64,56},{72,6... | collective-permute-start | bytes 1572872 | tf_op jit(solution)/shard_map/ppermute | solution.py:15
  334.6 26.9 %all-to-all-start = ((bf16[8,1024,128]{1,2,0:T(8,128)(2,1)}), bf16[8,1024,128]{1,2,0:T(8,128)(2,1)}, u32[]{:S(2)}, u32[]{:S(2)}) async-start(bf16[8,1024,128]{1,2,0:T(8,128)(2,1)} %stack.36), calls=%async_computation | async-start | bytes 4194304 | tf_op jit(solution)/shard_map/all_to_all | solution.py:131
  341.0 77.5 %all-gather.9.cloned.1.call-start = ((), (), s32[]{:S(2)}) async-start(), calls=%async_computation.7 | async-start | bytes 2359296 | tf_op jit(solution)/shard_map/all_gather | solution.py:141
  341.8 171.2 %reduce-scatter.17.cloned.1.call-start = ((), (), s32[]{:S(2)}) async-start(), calls=%async_computation.10 | async-start | bytes 1622016
  366.3 238.3 %reduce-scatter.19.cloned.1.call-start = ((), (), s32[]{:S(2)}) async-start(), calls=%async_computation.11 | async-start | bytes 1622016
  (32 other events, 101.4 us)
Sparse Core Ops, SparseCore 0:
  10.6 55.9 all-gather.4
  69.1 50.2 all-gather.6
  122.0 50.5 reduce-scatter.12
  175.0 54.3 reduce-scatter.14
  343.8 74.6 all-gather.8
  422.2 90.7 reduce-scatter.16
  516.9 87.6 reduce-scatter.18
